TPU v7x, 32 devices: a whole 2x2x4 slice. The times are simulated.
32 devices in a mesh: expert: 8 (over z, y), layer: 4 (over x, core).
Axes of the slice: x: 2, y: 2, z: 4, core: 2. Of those that a mesh axis runs over, the one named last changes fastest.
Arguments:
- gradient: bfloat16 [32, 16, 1536], P(('layer', 'expert')), parts along dimension 0, may hold values from -80 to 80
- prior_stat: float32 [32, 8], P('layer'), parts along dimension 0, may hold values from -600 to 600, as said below
Outputs:
- update: bfloat16 [32, 16, 1536], P(('layer', 'expert')), parts along dimension 0
- statistic: float32 [32, 8], P('layer'), parts along dimension 0
There are 4 independent parts, one for each index of `layer`. A program takes and returns all parts, laid end to end along the dimension named above; each array names one. Nothing has to cross between parts.
Inputs may be any that keep to these rules, and one draw needn't show every extreme that they name: `prior_stat`: symmetric positive definite.
All inputs are finite; a program needn't handle non-finite values.
Results may differ from a plain program's by a relative error of at most 0.001.
The roundings to bfloat16 on the way count: a program that leaves them out, or rounds other values in their place, can miss the bound.
Values may be sent and summed in bfloat16 or wider, within the bound.
A program may use at most 64 MiB of HBM per device.

v0:
```python
import jax
import jax.numpy as jnp
from jax import lax
from jax.sharding import PartitionSpec as P

ITERS = 5
ridge_rate = 0.001
energy_floor = 1e-06


def matmul_high(left, right):
    return jnp.dot(left, right, precision=lax.Precision.HIGHEST, preferred_element_type=jnp.float32)


def inverse_root(statistic):
    count_rows = statistic.shape[0]
    identity = jnp.eye(count_rows, dtype=jnp.float32)
    ridge_term = ridge_rate * jnp.trace(statistic) / count_rows
    shifted = statistic + ridge_term * identity
    start_scale = 2.5 / jnp.sqrt(jnp.sum(shifted * shifted))
    matrix = start_scale * shifted
    root = start_scale**0.25 * identity
    for repeat in range(ITERS):
        factor = 1.25 * identity - 0.25 * matrix
        root = matmul_high(root, factor)
        square = matmul_high(factor, factor)
        matrix = matmul_high(matmul_high(square, square), matrix)
    return root


def apply_graft(mixed_bf, graft):
    fenced = lax.optimization_barrier(mixed_bf)
    return (graft * fenced.astype(jnp.float32)).astype(jnp.bfloat16)


def slice_grams(pieces):
    grams = jnp.einsum("eqrf,gqrf->eqrg", pieces, pieces, preferred_element_type=jnp.float32)
    return (pieces, grams)


def body(gradient, prior_stat):
    experts = prior_stat.shape[0]
    owners = lax.axis_size("expert")
    local_experts = gradient.shape[0]
    slab_rows = gradient.shape[1]
    width = gradient.shape[2]
    entry_count = slab_rows * width
    slice_rows = slab_rows // owners
    blocked = gradient.reshape(local_experts, owners, slice_rows, width)
    regrouped, row_grams = slice_grams(
        lax.all_to_all(blocked, "expert", split_axis=1, concat_axis=0, tiled=True)
    )
    summed = lax.psum(jnp.sum(row_grams, axis=(1, 2)), "expert")
    gram_mean = summed / entry_count
    statistic = prior_stat + gram_mean
    root_bf = inverse_root(statistic).astype(jnp.bfloat16)
    flattened = regrouped.reshape(experts, -1)
    products = jnp.dot(root_bf, flattened, preferred_element_type=jnp.float32)
    mixed_bf = products.astype(jnp.bfloat16).reshape(experts, slice_rows, width)
    root_wide = root_bf.astype(jnp.float32)
    update_energy = jnp.sum(matmul_high(root_wide, gram_mean) * root_wide) / experts
    grad_energy = jnp.trace(gram_mean) / experts
    graft = jnp.sqrt((grad_energy + energy_floor) / (update_energy + energy_floor))
    grafted = apply_graft(mixed_bf, graft)
    update = lax.all_to_all(grafted, "expert", split_axis=0, concat_axis=1, tiled=True)
    return (update, statistic)


def solution(mesh):
    placed = (P(("layer", "expert"), None, None), P("layer", None))
    return jax.shard_map(
        body,
        mesh=mesh,
        in_specs=placed,
        out_specs=(P(("layer", "expert"), None, None), P("layer", None)),
        check_vma=False,
    )
```

profile of v0, /device:TPU:0, one launch (start us, length us, event | category | flops | bytes accessed | tf_op | source)
XLA Modules:
  0.0 50.7 jit_solution(7048645987614553434)
XLA Ops:
  0.6 0.8 %reshape.28 = bf16[1,8,2,1536]{3,2,1,0:T(2,128)(2,1)S(1)} reshape(bf16[1,16,1536]{2,1,0:T(8,128)(2,1)} %param.2) | data formatting | bytes 98304 | tf_op jit(solution)/shard_map/reshape | solution.py:49
  1.5 13.9 %all_to_all.21 = bf16[1,8,2,1536]{3,2,0,1:T(2,128)(2,1)S(1)} all-to-all(bf16[1,8,2,1536]{3,2,0,1:T(2,128)(2,1)S(1)} %bitcast.37), channel_id=1, replica_groups=mesh['expert'=8,'layer'=4] {'expert'}, dimensions={1} | all-to-all | bytes 98304 | tf_op jit(solution)/shard_map/all_to_all | solution.py:51
  15.4 0.1 convolution_bitcast_fusion
  15.5 0.0 copy-start.1
  15.5 18.0 %psum.7 = f32[8,8]{1,0:T(8,128)S(1)} all-reduce(f32[8,8]{1,0:T(8,128)S(1)} %convolution_bitcast_fusion), channel_id=1, replica_groups=mesh['expert'=8,'layer'=4] {'expert'}, use_global_device_ids=true, to_apply=%region_0.0 | all-reduce | flops 64 | bytes 512 | tf_op jit(solution)/shard_map/psum | solution.py:53
  33.5 0.0 copy-done.1
  33.5 0.7 %select_reduce_fusion = (f32[]{:T(128)}, f32[8,8]{1,0:T(8,128)S(1)}, f32[]{:T(128)}) fusion(f32[8,8]{1,0:T(8,128)S(1)} %copy-done.1, f32[8,8]{1,0:T(8,128)S(1)} %psum.7), kind=kLoop, calls=%fused_computation.18 | loop fusion | flops 446 | bytes 776 | tf_op jit(solution)/shard_map/jit(trace)/reduce_sum | solution.py:18
  34.2 0.0 copy-start
  34.8 0.6 %multiply_reduce_fusion = f32[]{:T(128)} fusion(f32[8,8]{1,0:T(8,128)S(1)} %get-tuple-element.3, f32[]{:T(128)S(6)} %div.24), kind=kLoop, calls=%fused_computation.16 | loop fusion | flops 319 | bytes 264 | tf_op jit(solution)/shard_map/reduce_sum | solution.py:20
  36.1 0.1 fusion.15
  36.3 0.1 fusion.4
  36.5 0.1 fusion.71
  36.6 0.0 copy-done
  36.6 0.1 fusion.6
  36.7 0.1 fusion.9
  36.9 0.1 fusion.10
  37.0 0.1 fusion.72
  37.1 0.1 fusion.73
  37.3 0.1 fusion.11
  37.4 0.1 fusion.12
  37.5 0.1 fusion.74
  37.7 0.1 fusion.75
  37.8 0.1 fusion.13
  38.0 0.1 fusion.14
  38.1 0.1 fusion.76
  38.2 0.1 fusion
  38.4 0.1 convolution_convert_fusion.1
  38.5 0.7 %fusion.1 = f32[]{:T(128)} fusion(bf16[8,8]{1,0:T(8,128)(2,1)S(1)} %convolution_convert_fusion.1, f32[8,8]{1,0:T(8,128)S(1)} %psum.7), kind=kOutput, calls=%fused_computation.6 | convolution fusion | flops 6399 | bytes 388 | tf_op jit(solution)/shard_map/dot_general | solution.py:12
  40.7 0.1 convolution_convert_fusion
  40.9 9.2 %all_to_all.22 = bf16[8,2,1536]{2,1,0:T(2,128)(2,1)S(1)} all-to-all(bf16[8,2,1536]{2,1,0:T(2,128)(2,1)S(1)} %copy.12), channel_id=1, replica_groups=mesh['expert'=8,'layer'=4] {'expert'}, dimensions={0} | all-to-all | bytes 98304 | tf_op jit(solution)/shard_map/all_to_all | solution.py:65
  50.1 0.6 %all_to_all.8 = bf16[1,16,1536]{2,1,0:T(8,128)(2,1)} reshape(bf16[8,2,1536]{2,1,0:T(2,128)(2,1)S(1)} %all_to_all.22) | data formatting | bytes 98304 | tf_op jit(solution)/shard_map/all_to_all | solution.py:65
  (3 shorter events, 0.1 us)
Async XLA Ops:
  15.5 18.0 %copy-start.1 = (f32[8,8]{1,0:T(8,128)S(1)}, f32[8,8]{1,0:T(8,128)}, u32[]{:S(2)}) copy-start(f32[8,8]{1,0:T(8,128)} %param.3) | copy-start | bytes 772
  34.2 2.4 %copy-start = (f32[8,8]{1,0:T(8,128)}, f32[8,8]{1,0:T(8,128)S(1)}, u32[]{:S(2)}) copy-start(f32[8,8]{1,0:T(8,128)S(1)} %get-tuple-element.3) | copy-start | bytes 772
where the time goes:
time: 51 us; the launch traced here: 50.7 us
  blocking collectives  41.1 us (81%)
  between operations  3.51 us (7%)
  matrix products  3.31 us (6%)
  local copies, waits for them, and re-layouts  1.52 us (3%)
  other arithmetic  1.3 us (3%)
    psum x1, blocking collectives, body(): summed = lax.psum(jnp.sum(row_grams, axis=(1, 2)), 'expert')  18 us
    all_to_all x1, blocking collectives, body(): lax.all_to_all(blocked, 'expert', split_axis=1, concat_axis=0, tiled=True)  13.9 us
    all_to_all x1, blocking collectives, body(): lax.all_to_all(grafted, 'expert', split_axis=0, concat_axis=1, tiled=True)  9.17 us
    dot_general x18, matrix products, matmul_high(): jnp.dot(left, right, precision=lax.Precision.HIGHEST, preferred_element_t...  3.05 us

commit v1 on v0

--- a/solution.py
+++ b/solution.py
@@ -50,7 +50,7 @@
     regrouped, row_grams = slice_grams(
         lax.all_to_all(blocked, "expert", split_axis=1, concat_axis=0, tiled=True)
     )
-    summed = lax.psum(jnp.sum(row_grams, axis=(1, 2)), "expert")
+    summed = jnp.sum(lax.all_gather(jnp.sum(row_grams, axis=(1, 2)), "expert"), axis=0)
     gram_mean = summed / entry_count
     statistic = prior_stat + gram_mean
     root_bf = inverse_root(statistic).astype(jnp.bfloat16)

time: 51 us -> 64.3 us (1.26)
  blocking collectives: 41.1 us -> 53.7 us
  local copies, waits for them, and re-layouts: 1.52 us -> 2.19 us
    all_gather x0 -> x1, blocking collectives: none -> 30.6 us  [body(): lax.all_gather(jnp.sum(row_grams, axis=(1, 2)), 'expert')]
    psum x1 -> x0, blocking collectives: 18 us -> none  [body(): summed = lax.psum(jnp.sum(row_grams, axis=(1, 2)), 'expert')]
    unnamed x5, local copies, waits for them, and re-layouts: 0.02 us -> 0.69 us
where the time goes in v1:
time: 64.3 us; the launch traced here: 64 us
  blocking collectives  53.7 us (84%)
  between operations  3.51 us (5%)
  matrix products  3.31 us (5%)
  local copies, waits for them, and re-layouts  2.19 us (3%)
  other arithmetic  1.31 us (2%)
    all_gather x1, blocking collectives, body(): lax.all_gather(jnp.sum(row_grams, axis=(1, 2)), 'expert')  30.6 us
    all_to_all x1, blocking collectives, body(): lax.all_to_all(blocked, 'expert', split_axis=1, concat_axis=0, tiled=True)  13.9 us
    all_to_all x1, blocking collectives, body(): lax.all_to_all(grafted, 'expert', split_axis=0, concat_axis=1, tiled=True)  9.17 us
    dot_general x18, matrix products, matmul_high(): jnp.dot(left, right, precision=lax.Precision.HIGHEST, preferred_element_t...  3.05 us

profile of v1, /device:TPU:0, one launch (start us, length us, event | category | flops | bytes accessed | tf_op | source)
XLA Modules:
  0.0 64.0 jit_solution(16664513255025962189)
XLA Ops:
  0.6 0.8 %reshape.28 = bf16[1,8,2,1536]{3,2,1,0:T(2,128)(2,1)S(1)} reshape(bf16[1,16,1536]{2,1,0:T(8,128)(2,1)} %param.2) | data formatting | bytes 98304 | tf_op jit(solution)/shard_map/reshape | solution.py:49
  1.5 13.9 %all_to_all.21 = bf16[1,8,2,1536]{3,2,0,1:T(2,128)(2,1)S(1)} all-to-all(bf16[1,8,2,1536]{3,2,0,1:T(2,128)(2,1)S(1)} %bitcast.39), channel_id=1, replica_groups=mesh['expert'=8,'layer'=4] {'expert'}, dimensions={1} | all-to-all | bytes 98304 | tf_op jit(solution)/shard_map/all_to_all | solution.py:51
  15.4 0.1 convolution_bitcast_fusion
  15.5 30.6 %all-gather = f32[64,8]{1,0:T(8,128)S(1)} all-gather(f32[8,8]{1,0:T(8,128)S(1)} %convolution_bitcast_fusion), channel_id=2, replica_groups=mesh['expert'=8,'layer'=4] {'expert'}, dimensions={0}, use_global_device_ids=true | all-gather | bytes 2304 | tf_op jit(solution)/shard_map/all_gather | solution.py:53
  46.1 0.0 copy-start.1
  46.1 0.7 %copy-done.1 = f32[8,8]{1,0:T(8,128)S(1)} copy-done((f32[8,8]{1,0:T(8,128)S(1)}, f32[8,8]{1,0:T(8,128)}, u32[]{:S(2)}) %copy-start.1) | copy-done | bytes 280
  46.8 0.7 %select_reduce_fusion = (f32[]{:T(128)}, f32[8,8]{1,0:T(8,128)S(1)}, f32[]{:T(128)}) fusion(f32[8,8]{1,0:T(8,128)S(1)} %copy-done.1, f32[8,8]{1,0:T(8,128)S(1)} %bitcast_reduce_fusion), kind=kLoop, calls=%fused_computation.19 | loop fusion | flops 446 | bytes 776 | tf_op jit(solution)/shard_map/jit(trace)/reduce_sum | solution.py:18
  47.5 0.0 copy-start
  48.1 0.6 multiply_reduce_fusion
  49.4 0.1 fusion.15
  49.6 0.1 fusion.4
  49.7 0.1 fusion.71
  49.9 0.0 copy-done
  49.9 0.1 fusion.6
  50.0 0.1 fusion.9
  50.2 0.1 fusion.10
  50.3 0.1 fusion.72
  50.4 0.1 fusion.73
  50.6 0.1 fusion.11
  50.7 0.1 fusion.12
  50.8 0.1 fusion.74
  51.0 0.1 fusion.75
  51.1 0.1 fusion.13
  51.3 0.1 fusion.14
  51.4 0.1 fusion.76
  51.5 0.1 fusion
  51.7 0.1 convolution_convert_fusion.1
  51.8 0.7 %fusion.1 = f32[]{:T(128)} fusion(bf16[8,8]{1,0:T(8,128)(2,1)S(1)} %convolution_convert_fusion.1, f32[8,8]{1,0:T(8,128)S(1)} %bitcast_reduce_fusion), kind=kOutput, calls=%fused_computation.6 | convolution fusion | flops 6399 | bytes 388 | tf_op jit(solution)/shard_map/dot_general | solution.py:12
  54.0 0.1 convolution_convert_fusion
  54.2 9.2 %all_to_all.22 = bf16[8,2,1536]{2,1,0:T(2,128)(2,1)S(1)} all-to-all(bf16[8,2,1536]{2,1,0:T(2,128)(2,1)S(1)} %copy.12), channel_id=1, replica_groups=mesh['expert'=8,'layer'=4] {'expert'}, dimensions={0} | all-to-all | bytes 98304 | tf_op jit(solution)/shard_map/all_to_all | solution.py:65
  63.4 0.6 %all_to_all.8 = bf16[1,16,1536]{2,1,0:T(8,128)(2,1)} reshape(bf16[8,2,1536]{2,1,0:T(2,128)(2,1)S(1)} %all_to_all.22) | data formatting | bytes 98304 | tf_op jit(solution)/shard_map/all_to_all | solution.py:65
  (4 shorter events, 0.1 us)
Async XLA Ops:
  46.1 0.7 %copy-start.1 = (f32[8,8]{1,0:T(8,128)S(1)}, f32[8,8]{1,0:T(8,128)}, u32[]{:S(2)}) copy-start(f32[8,8]{1,0:T(8,128)} %param.3) | copy-start | bytes 772
  47.5 2.4 %copy-start = (f32[8,8]{1,0:T(8,128)}, f32[8,8]{1,0:T(8,128)S(1)}, u32[]{:S(2)}) copy-start(f32[8,8]{1,0:T(8,128)S(1)} %get-tuple-element.3) | copy-start | bytes 772
